TPU v7x, 128 devices: a whole 4x4x4 slice. The times are simulated.
128 devices in a mesh: fsdp: 16 (over x, y), dp: 8 (over z, core).
Axes of the slice: x: 4, y: 4, z: 4, core: 2. Of those that a mesh axis runs over, the one named last changes fastest.
Arguments:
- tokens: bfloat16 [32768, 960], P(('fsdp', 'dp')), may hold values from -6 to 6
- layer_weights: bfloat16 [1, 960, 10240], P(None, None, ('fsdp', 'dp'))
- norm_gains: bfloat16 [1, 1920], P(None, ('fsdp', 'dp')), may hold values from 0.5 to 1.5
- seq_ids: int32 [32768], P(('fsdp', 'dp')), may hold values from 0 to 255, as said below
- out_grad: bfloat16 [32768, 960], P(('fsdp', 'dp')), may hold values from -6 to 6
Outputs:
- activations: bfloat16 [32768, 960], P(('fsdp', 'dp'))
- input_grad: float32 [32768, 960], P(('fsdp', 'dp'))
- weight_grad: float32 [1, 960, 10240], P(None, None, ('fsdp', 'dp'))
- gain_grad: float32 [1, 1920], P(None, ('fsdp', 'dp'))
Inputs may be any that keep to these rules, and one draw needn't show every extreme that they name: `seq_ids`: within each device's 256 rows: 0 in the first row, never falling, rising by at most one from a row to the next, so every sequence lies whole on one device; on some device all rows form one sequence, on another every row is a sequence of its own.
All inputs are finite; a program needn't handle non-finite values.
Results may differ from a plain program's by a relative error of at most 0.013.
Values may be sent and summed in bfloat16 or wider, within the bound.
A program may use at most 256 MiB of HBM per device.

v0:
```python
import jax
import jax.numpy as jnp
from jax import lax
from jax.sharding import PartitionSpec as P

QUERY_HEADS = 15
KEY_VALUE_HEADS = 5
HEAD_SIZE = 64
epsilon = 1e-05
rope_base = 100000.0


def mix_heads(pattern, left, right):
    return jnp.einsum(pattern, left, right, preferred_element_type=jnp.float32)


def across(left, right):
    return lax.dot_general(
        left, right, (((0,), (0,)), ((), ())), preferred_element_type=jnp.float32
    )


def against(left, right):
    return lax.dot_general(
        left, right, (((1,), (1,)), ((), ())), preferred_element_type=jnp.float32
    )


def tables(block_ids, head_width):
    sequence_length = block_ids.shape[0]
    row_index = jnp.arange(sequence_length, dtype=jnp.int32)
    same_seq = block_ids[:, None] == block_ids[None, :]
    seq_start = jnp.min(jnp.where(same_seq, row_index[None, :], sequence_length), axis=1)
    position = (row_index - seq_start).astype(jnp.float32)
    inv_freq = rope_base ** (-jnp.arange(0, head_width, 2).astype(jnp.float32) / head_width)
    angles = position[:, None] * inv_freq[None, :]
    allowed = same_seq & (row_index[None, :] <= row_index[:, None])
    return (jnp.cos(angles)[:, None, :], jnp.sin(angles)[:, None, :], allowed)


def apply_rotary(values, cosine_table, sine_table, direction):
    half_dim = values.shape[-1] // 2
    a = values[..., :half_dim]
    b = values[..., half_dim:]
    return jnp.concatenate(
        [
            a * cosine_table - direction * b * sine_table,
            b * cosine_table + direction * a * sine_table,
        ],
        axis=-1,
    )


def norm_forward(values, gain):
    inv_rms = lax.rsqrt(jnp.mean(values * values, axis=-1, keepdims=True) + epsilon)
    return (inv_rms, (values * inv_rms * gain).astype(jnp.bfloat16))


def norm_backward(d_norm, values, inv_rms, gain):
    u = d_norm * gain
    d_gain = jnp.sum(d_norm * values * inv_rms, axis=0)
    d_values = inv_rms * u - values * inv_rms**3 * jnp.mean(u * values, axis=-1, keepdims=True)
    return (d_values, d_gain)


def widths(weight_tree, cosine_table):
    head_width = cosine_table.shape[-1] * 2
    query_width = QUERY_HEADS * head_width
    key_value_width = KEY_VALUE_HEADS * head_width
    perceptron_begin = 2 * query_width + 2 * key_value_width
    hidden_width = (weight_tree.shape[1] - perceptron_begin) // 3
    return (head_width, query_width, key_value_width, perceptron_begin, hidden_width)


def scores(query_rows, key_rows, allowed, head_width):
    score_vals = mix_heads("tkgd,skd->kgts", query_rows, key_rows) * head_width ** (-0.5)
    return jnp.where(allowed, score_vals, -1e30)


def layer_forward(stream, weight_tree, gain_row, cosine_table, sine_table, allowed):
    head_width, query_width, key_value_width, perceptron_begin, hidden_width = widths(
        weight_tree, cosine_table
    )
    width = stream.shape[1]
    sequence_length = stream.shape[0]
    head_group = QUERY_HEADS // KEY_VALUE_HEADS
    gain_a = gain_row[:width].astype(jnp.float32)
    gain_b = gain_row[width:].astype(jnp.float32)
    rms_a, normed_a = norm_forward(stream, gain_a)
    query_key_value = jnp.dot(
        normed_a,
        weight_tree[:, : query_width + 2 * key_value_width],
        preferred_element_type=jnp.float32,
    )
    query_rows = (
        apply_rotary(
            query_key_value[:, :query_width].reshape(sequence_length, QUERY_HEADS, head_width),
            cosine_table,
            sine_table,
            1.0,
        )
        .astype(jnp.bfloat16)
        .reshape(sequence_length, KEY_VALUE_HEADS, head_group, head_width)
    )
    key_rows = apply_rotary(
        query_key_value[:, query_width : query_width + key_value_width].reshape(
            sequence_length, KEY_VALUE_HEADS, head_width
        ),
        cosine_table,
        sine_table,
        1.0,
    ).astype(jnp.bfloat16)
    value_rows = (
        query_key_value[:, query_width + key_value_width : query_width + 2 * key_value_width]
        .reshape(sequence_length, KEY_VALUE_HEADS, head_width)
        .astype(jnp.bfloat16)
    )
    score_vals = scores(query_rows, key_rows, allowed, head_width)
    row_max = jnp.max(score_vals, axis=-1, keepdims=True)
    expon = jnp.exp(score_vals - row_max)
    row_sum = jnp.sum(expon, axis=-1, keepdims=True)
    log_total = row_max + jnp.log(row_sum)
    attended = (
        mix_heads("kgts,skd->tkgd", (expon / row_sum).astype(jnp.bfloat16), value_rows)
        .reshape(sequence_length, query_width)
        .astype(jnp.bfloat16)
    )
    middle = stream + against(
        attended, weight_tree[:, query_width + 2 * key_value_width : perceptron_begin]
    )
    rms_b, normed_b = norm_forward(middle, gain_b)
    gate_up = jnp.dot(
        normed_b,
        weight_tree[:, perceptron_begin : perceptron_begin + 2 * hidden_width],
        preferred_element_type=jnp.float32,
    )
    gate_val = gate_up[:, :hidden_width]
    upward = gate_up[:, hidden_width:]
    hidden = (jax.nn.silu(gate_val) * upward).astype(jnp.bfloat16)
    result = middle + against(hidden, weight_tree[:, perceptron_begin + 2 * hidden_width :])
    return (
        result,
        (
            stream,
            rms_a,
            normed_a,
            query_rows,
            key_rows,
            value_rows,
            log_total,
            attended,
            middle,
            rms_b,
            normed_b,
            gate_val,
            upward,
            hidden,
        ),
    )


def layer_backward(upstream, saved_acts, weight_tree, gain_row, cosine_table, sine_table, allowed):
    (
        stream,
        rms_a,
        normed_a,
        query_rows,
        key_rows,
        value_rows,
        log_total,
        attended,
        middle,
        rms_b,
        normed_b,
        gate_val,
        upward,
        hidden,
    ) = saved_acts
    head_width, query_width, key_value_width, perceptron_begin, hidden_width = widths(
        weight_tree, cosine_table
    )
    width = stream.shape[1]
    sequence_length = stream.shape[0]
    head_group = QUERY_HEADS // KEY_VALUE_HEADS
    gain_a = gain_row[:width].astype(jnp.float32)
    gain_b = gain_row[width:].astype(jnp.float32)
    out_rounded = upstream.astype(jnp.bfloat16)
    d_hidden = jnp.dot(
        out_rounded,
        weight_tree[:, perceptron_begin + 2 * hidden_width :],
        preferred_element_type=jnp.float32,
    )
    d_down = across(out_rounded, hidden)
    sig_gate = jax.nn.sigmoid(gate_val)
    d_gate = d_hidden * upward * sig_gate * (1.0 + gate_val * (1.0 - sig_gate))
    d_upward = d_hidden * gate_val * sig_gate
    d_gate_up = jnp.concatenate([d_gate, d_upward], axis=1).astype(jnp.bfloat16)
    d_normed_b = against(
        d_gate_up, weight_tree[:, perceptron_begin : perceptron_begin + 2 * hidden_width]
    )
    d_gate_up_w = across(normed_b, d_gate_up)
    d_mid_norm, d_gain_b = norm_backward(d_normed_b, middle, rms_b, gain_b)
    d_middle = upstream + d_mid_norm
    middle_cast = d_middle.astype(jnp.bfloat16)
    attended_gradient = (
        jnp.dot(
            middle_cast,
            weight_tree[:, query_width + 2 * key_value_width : perceptron_begin],
            preferred_element_type=jnp.float32,
        )
        .astype(jnp.bfloat16)
        .reshape(sequence_length, KEY_VALUE_HEADS, head_group, head_width)
    )
    d_out_w = across(middle_cast, attended)
    expon = jnp.exp(scores(query_rows, key_rows, allowed, head_width) - log_total)
    d_v = mix_heads("kgts,tkgd->skd", expon.astype(jnp.bfloat16), attended_gradient)
    d_p = mix_heads("tkgd,skd->kgts", attended_gradient, value_rows)
    d_s = expon * (d_p - jnp.sum(expon * d_p, axis=-1, keepdims=True))
    d_s_rounded = (d_s * head_width ** (-0.5)).astype(jnp.bfloat16)
    d_q = mix_heads("kgts,skd->tkgd", d_s_rounded, key_rows).reshape(
        sequence_length, QUERY_HEADS, head_width
    )
    d_k = mix_heads("kgts,tkgd->skd", d_s_rounded, query_rows)
    d_q = apply_rotary(d_q, cosine_table, sine_table, -1.0).reshape(sequence_length, query_width)
    d_k = apply_rotary(d_k, cosine_table, sine_table, -1.0).reshape(
        sequence_length, key_value_width
    )
    d_qkv = jnp.concatenate(
        [d_q, d_k, d_v.reshape(sequence_length, key_value_width)], axis=1
    ).astype(jnp.bfloat16)
    d_normed_a = against(d_qkv, weight_tree[:, : query_width + 2 * key_value_width])
    d_qkv_w = across(normed_a, d_qkv)
    d_in_norm, d_gain_a = norm_backward(d_normed_a, stream, rms_a, gain_a)
    d_stream = d_middle + d_in_norm
    weight_part = jnp.concatenate([d_qkv_w, d_out_w, d_gate_up_w, d_down], axis=1)
    return (d_stream, weight_part, jnp.concatenate([d_gain_a, d_gain_b]))


def body(tokens, layer_weights, norm_gains, seq_ids, out_grad):
    layer_count = layer_weights.shape[0]
    cosine_table, sine_table, allowed = tables(seq_ids, HEAD_SIZE)
    stream = tokens.astype(jnp.float32)
    held_list = []
    layer = 0
    gathered = lax.all_gather(layer_weights[layer], ("fsdp", "dp"), axis=1, tiled=True)
    gain_row = lax.all_gather(norm_gains[layer], ("fsdp", "dp"), axis=0, tiled=True)
    held_list.append((gathered, gain_row))
    stream, saved_acts = layer_forward(
        stream, gathered, gain_row, cosine_table, sine_table, allowed
    )
    saved_list = [saved_acts]
    upstream = out_grad.astype(jnp.float32)
    weight_parts = [None] * layer_count
    gain_parts = [None] * layer_count
    for layer in reversed(range(layer_count)):
        gathered, gain_row = (
            lax.all_gather(layer_weights[layer], ("fsdp", "dp"), axis=1, tiled=True),
            lax.all_gather(norm_gains[layer], ("fsdp", "dp"), axis=0, tiled=True),
        )
        upstream, weight_term, gain_term = layer_backward(
            upstream, saved_list[layer], gathered, gain_row, cosine_table, sine_table, allowed
        )
        weight_parts[layer], gain_parts[layer] = (
            lax.psum_scatter(weight_term, ("fsdp", "dp"), scatter_dimension=1, tiled=True),
            lax.psum_scatter(gain_term, ("fsdp", "dp"), scatter_dimension=0, tiled=True),
        )
    weight_grad = jnp.stack(weight_parts)
    gain_grad = jnp.stack(gain_parts)
    return (stream.astype(jnp.bfloat16), upstream, weight_grad, gain_grad)


def solution(mesh):
    return jax.shard_map(
        body,
        mesh=mesh,
        in_specs=(
            P(("fsdp", "dp"), None),
            P(None, None, ("fsdp", "dp")),
            P(None, ("fsdp", "dp")),
            P(("fsdp", "dp")),
            P(("fsdp", "dp"), None),
        ),
        out_specs=(
            P(("fsdp", "dp"), None),
            P(("fsdp", "dp"), None),
            P(None, None, ("fsdp", "dp")),
            P(None, ("fsdp", "dp")),
        ),
        check_vma=False,
    )
```

profile of v0, /device:TPU:0, one launch (start us, length us, event | category | flops | bytes accessed | tf_op | source)
XLA Modules:
  0.0 977.7 jit_solution(9443763462687554647)
XLA Ops:
  7.2 0.7 all-gather.4.cloned.1.call-update
  8.0 0.9 dynamic-update-slice
  8.8 68.9 %all-reduce = bf16[1920]{0:T(1024)(128)(2,1)S(1)} all-reduce(bf16[1920]{0:T(1024)(128)(2,1)S(1)} %dynamic-update-slice), channel_id=2, replica_groups=mesh['fsdp'=16,'dp'=8] {'fsdp','dp'}, use_global_device_ids=true, to_apply=%add | all-reduce | flops 1920 | bytes 7680
  77.8 0.9 fusion.59
  78.7 1.2 fusion.49
  80.0 0.9 compare_and_fusion
  81.0 19.9 %all-gather.4.cloned.1.call-done = bf16[1,960,10240]{1,2,0:T(8,128)(2,1)} async-done(((bf16[1,960,80]{1,2,0:T(8,128)(2,1)}), bf16[1,960,10240]{1,2,0:T(8,128)(2,1)}) %all-gather.4.cloned.1.call-update) | async-done | bytes 19660816 | tf_op jit(solution)/shard_map/all_gather | solution.py:245
  100.9 3.1 fusion.16
  104.5 0.8 fusion.76
  105.9 0.8 fusion.38
  107.2 2.5 multiply_reduce_fusion.2
  109.7 9.5 fusion.3
  119.3 8.5 multiply_convert_fusion.1
  127.7 8.7 multiply_reduce_fusion
  136.7 2.2 fusion.39
  139.0 2.6 fusion.77
  141.6 0.7 fusion.46
  142.3 8.1 fusion.42
  150.5 8.2 fusion.23
  158.7 3.8 fusion.60
  162.5 8.2 fusion.29
  170.9 5.2 convolution_bitcast_fusion
  176.1 3.8 fusion.58
  179.9 41.2 %concatenate.43 = f32[960,10240]{1,0:T(8,128)} concatenate(f32[960,1600]{1,0:T(8,128)} %fusion.58, f32[960,960]{1,0:T(8,128)} %fusion.60, f32[960,5120]{1,0:T(8,128)} %fusion.29, f32[960,2560]{1,0:T(8,128)} %convolution_bitcast_fusion), dimensions={1} | concatenate | bytes 78643200 | tf_op jit(solution)/shard_map/concatenate | solution.py:235
  221.1 40.9 %copy.27 = f32[960,10240]{0,1:T(8,128)} copy(f32[960,10240]{1,0:T(8,128)} %concatenate.43) | data formatting | bytes 78643200
  262.0 4.4 fusion.57
  266.5 70.4 %all-reduce.1 = f32[1920]{0:T(1024)S(1)} all-reduce(f32[1920]{0:T(1024)S(1)} %pad_maximum_fusion.11), channel_id=5, replica_groups=mesh['fsdp'=16,'dp'=8] {'fsdp','dp'}, use_global_device_ids=true, to_apply=%region_11.12.clone | all-reduce | flops 1920 | bytes 15360
  337.5 2.4 fusion.54
  339.9 5.8 fusion.35
  345.7 623.0 %reduce-scatter.4.cloned.1.call-done = f32[80,960]{1,0:T(8,128)} async-done(((f32[10240,960]{1,0:T(8,128)}), f32[80,960]{1,0:T(8,128)}) %reduce-scatter.4.cloned.1.call-update) | async-done | bytes 307216
  968.7 1.2 copy.28
  969.9 0.9 copy.18
  (59 shorter events, 3.1 us)
Async XLA Ops:
  7.2 93.8 %all-gather.4.cloned.1.call-start = ((), (), s32[]{:S(2)}) async-start(), calls=%async_computation.1 | async-start | bytes 21135360 | tf_op jit(solution)/shard_map/all_gather | solution.py:245
  7.9 960.8 %reduce-scatter.4.cloned.1.call-start = ((), (), s32[]{:S(2)}) async-start(), calls=%async_computation.2 | async-start | bytes 42270720
  104.4 1.4 copy-start.11
  104.4 1.4 copy-start.12
  104.4 1.4 copy-start.14
  105.2 36.3 %copy-start = (f32[5,3,256,256]{2,3,1,0:T(8,128)}, f32[5,3,256,256]{2,3,1,0:T(8,128)S(1)}, u32[]{:S(2)}) copy-start(f32[5,3,256,256]{2,3,1,0:T(8,128)S(1)} %get-tuple-element.37) | copy-start | bytes 11796484
  105.8 1.4 copy-start.1
  106.6 3.1 copy-start.9
  109.7 9.5 copy-start.2
  127.7 8.7 copy-start.3
  127.7 8.7 copy-start.5
  142.3 8.2 copy-start.13
  158.7 3.8 copy-start.4
  158.7 3.8 copy-start.6
  162.5 8.2 copy-start.10
  162.5 8.3 copy-start.8
  162.5 8.4 copy-start.7
  262.0 4.4 copy-start.15
Sparse Core Ops, SparseCore 0:
  11.0 89.9 all-gather.3
  262.1 706.5 reduce-scatter.3
where the time goes:
time: 980 us; the launch traced here: 978 us
  waiting for transfers between devices  644 us (66%)
  blocking collectives  139 us (14%)
  matrix products  86.9 us (9%)
  local copies, waits for them, and re-layouts  86.4 us (9%)
  between operations  14.3 us (1%)
    unnamed x3, waiting for transfers between devices  624 us
    unnamed x2, blocking collectives  139 us
    unnamed x38, local copies, waits for them, and re-layouts  44.5 us
    concatenate x1, local copies, waits for them, and re-layouts, layer_backward(): jnp.concatenate([d_qkv_w, d_out_w, d_gate_up_w, d_down], axis=1)  41.2 us
    dot_general x4, matrix products, against(): lax.dot_general(left, right, (((1,), (1,)), ((), ())), preferred_element_...  21.4 us
    dot_general x6, matrix products, mix_heads(): return jnp.einsum(pattern, left, right, preferred_element_type=jnp.float32)  21.3 us
    dot_general x4, matrix products, across(): lax.dot_general(left, right, (((0,), (0,)), ((), ())), preferred_element_...  20.9 us
    all_gather x1, waiting for transfers between devices, body(): lax.all_gather(layer_weights[layer], ('fsdp', 'dp'), axis=1, tiled=True)  19.9 us
  transfers between devices with their start and end apart: 2, of which 2 were waited for; matrix products, arithmetic and copies ran while one was open for 2% of the time, Pallas kernels for 0%

commit v1 on v0

--- a/solution.py
+++ b/solution.py
@@ -242,7 +242,11 @@
     stream = tokens.astype(jnp.float32)
     held_list = []
     layer = 0
-    gathered = lax.all_gather(layer_weights[layer], ("fsdp", "dp"), axis=1, tiled=True)
+    own = layer_weights[layer]
+    size = lax.axis_size(("fsdp", "dp"))
+    pieces = jnp.stack([own for _ in range(size)])
+    pieces = lax.all_to_all(pieces, ("fsdp", "dp"), split_axis=0, concat_axis=0)
+    gathered = jnp.concatenate(pieces, axis=1)
     gain_row = lax.all_gather(norm_gains[layer], ("fsdp", "dp"), axis=0, tiled=True)
     held_list.append((gathered, gain_row))
     stream, saved_acts = layer_forward(

time: 980 us -> 1300 us (1.33)
  blocking collectives: 139 us -> 466 us
  waiting for transfers between devices: 644 us -> 624 us
    unnamed x2, blocking collectives: 139 us -> 466 us
    all_gather x1, waiting for transfers between devices: 19.9 us -> 0.01 us  [body(): lax.all_gather(layer_weights[layer], ('fsdp', 'dp'), axis=1, tiled=True)]
  transfers between devices with their start and end apart: 2 -> 3, of which waited for: 2 -> 1; matrix products, arithmetic and copies ran while one was open for 2% -> 3% of each run, Pallas kernels for 0% -> 0%
where the time goes in v1:
time: 1300 us
  waiting for transfers between devices  624 us (48%)
  blocking collectives  466 us (36%)
  local copies, waits for them, and re-layouts  93.7 us (7%)
  matrix products  86.6 us (7%)
  between operations  14.4 us (1%)
    unnamed x3, waiting for transfers between devices  624 us
    unnamed x2, blocking collectives  466 us
    unnamed x38, local copies, waits for them, and re-layouts  43.8 us
    concatenate x1, local copies, waits for them, and re-layouts, layer_backward(): jnp.concatenate([d_qkv_w, d_out_w, d_gate_up_w, d_down], axis=1)  41.2 us
  transfers between devices with their start and end apart: 3, of which 1 were waited for; matrix products, arithmetic and copies ran while one was open for 3% of the time, Pallas kernels for 0%

profile of v1, /device:TPU:0, one launch (start us, length us, event | category | flops | bytes accessed | tf_op | source)
XLA Modules:
  0.0 1301.2 jit_solution(12796143470656602817)
XLA Ops:
  7.2 0.7 all-gather.4.cloned.1.call-update
  7.9 8.0 stack.9
  15.9 11.6 all-to-all-start
  27.9 396.8 %all-reduce = bf16[1920]{0:T(1024)(128)(2,1)S(1)} all-reduce(bf16[1920]{0:T(1024)(128)(2,1)S(1)} %dynamic-update-slice), channel_id=2, replica_groups=mesh['fsdp'=16,'dp'=8] {'fsdp','dp'}, use_global_device_ids=true, to_apply=%add | all-reduce | flops 1920 | bytes 7680
  425.4 3.1 fusion.15
  428.9 0.8 fusion.76
  429.6 0.6 fusion.12
  430.2 0.8 fusion.38
  431.0 0.5 copy-done
  431.6 2.6 multiply_reduce_fusion.2
  434.3 9.5 fusion.3
  443.8 8.5 multiply_convert_fusion.1
  452.3 8.1 multiply_reduce_fusion
  460.7 2.4 fusion.39
  463.1 2.6 fusion.77
  465.7 0.7 fusion.46
  466.5 8.2 fusion.42
  474.7 8.2 fusion.27
  482.9 3.8 fusion.60
  486.7 8.2 fusion.29
  495.1 5.2 convolution_bitcast_fusion
  500.3 3.8 fusion.58
  504.1 41.2 %concatenate.43 = f32[960,10240]{1,0:T(8,128)} concatenate(f32[960,1600]{1,0:T(8,128)} %fusion.58, f32[960,960]{1,0:T(8,128)} %fusion.60, f32[960,5120]{1,0:T(8,128)} %fusion.29, f32[960,2560]{1,0:T(8,128)} %convolution_bitcast_fusion), dimensions={1} | concatenate | bytes 78643200 | tf_op jit(solution)/shard_map/concatenate | solution.py:235
  545.3 40.9 %copy.33 = f32[960,10240]{0,1:T(8,128)} copy(f32[960,10240]{1,0:T(8,128)} %concatenate.43) | data formatting | bytes 78643200
  586.2 4.4 fusion.57
  590.7 69.2 %all-reduce.1 = f32[1920]{0:T(1024)S(1)} all-reduce(f32[1920]{0:T(1024)S(1)} %pad_maximum_fusion.11), channel_id=5, replica_groups=mesh['fsdp'=16,'dp'=8] {'fsdp','dp'}, use_global_device_ids=true, to_apply=%region_11.12.clone | all-reduce | flops 1920 | bytes 15360
  659.9 0.6 dynamic-slice_bitcast_fusion
  660.5 2.4 fusion.54
  662.9 5.8 fusion.35
  668.7 623.6 %reduce-scatter.4.cloned.1.call-done = f32[80,960]{1,0:T(8,128)} async-done(((f32[10240,960]{1,0:T(8,128)}), f32[80,960]{1,0:T(8,128)}) %reduce-scatter.4.cloned.1.call-update) | async-done | bytes 307216
  1292.3 1.2 copy.34
  1293.5 0.9 copy.24
  (62 shorter events, 2.0 us)
Async XLA Ops:
  7.2 436.7 %all-gather.4.cloned.1.call-start = ((), (), s32[]{:S(2)}) async-start(), calls=%async_computation.2 | async-start | bytes 21135360 | tf_op jit(solution)/shard_map/all_gather | solution.py:261
  15.9 11.7 copy-start.15
  15.9 408.8 %copy-start.14 = (s32[256]{0:T(256)S(1)}, s32[256]{0:T(256)}, u32[]{:S(2)}) copy-start(s32[256]{0:T(256)} %param.8) | copy-start | bytes 3076
  15.9 409.0 %copy-start.2 = (bf16[256,960]{0,1:T(8,128)(2,1)S(1)}, bf16[256,960]{0,1:T(8,128)(2,1)}, u32[]{:S(2)}) copy-start(bf16[256,960]{0,1:T(8,128)(2,1)} %param.5) | copy-start | bytes 1474564
  15.9 409.5 %all-to-all-start = ((bf16[128,960,80]{1,2,0:T(8,128)(2,1)}), bf16[128,960,80]{1,2,0:T(8,128)(2,1)}, u32[]{:S(2)}, u32[]{:S(2)}) async-start(bf16[128,960,80]{1,2,0:T(8,128)(2,1)} %stack.9), calls=%async_computation | async-start | bytes 41943040 | tf_op jit(solution)/shard_map/all_to_all | solution.py:248
  27.5 1264.8 %reduce-scatter.4.cloned.1.call-start = ((), (), s32[]{:S(2)}) async-start(), calls=%async_computation.3 | async-start | bytes 42270720
  428.8 1.4 copy-start.12
  428.8 1.4 copy-start.13
  429.6 2.0 copy-start
  431.6 2.7 copy-start.10
  434.3 9.5 copy-start.3
  452.3 8.2 copy-start.4
  452.3 8.2 copy-start.6
  460.7 5.0 copy-start.1
  482.9 3.8 copy-start.5
  482.9 3.8 copy-start.7
  486.7 8.2 copy-start.11
  486.7 8.3 copy-start.9
  486.7 8.4 copy-start.8
Sparse Core Ops, SparseCore 0:
  11.0 351.8 all-gather.3
  586.3 705.9 reduce-scatter.3
